TPU v7x, 32 devices: a whole 2x2x4 slice. The times are simulated.
32 devices in a mesh: groups: 2 (over y), pages: 4 (over z), patches: 4 (over x, core).
Axes of the slice: x: 2, y: 2, z: 4, core: 2. Of those that a mesh axis runs over, the one named last changes fastest.
Arguments:
- queries: bfloat16 [16, 32, 128], P(('groups', 'pages'), 'patches'), parts along dimension 0, may hold values from -6 to 6
- gallery: bfloat16 [640, 1024, 128], P(('groups', 'pages'), 'patches'), parts along dimension 0, may hold values from -0.5 to 0.5
- page_rows: int32 [640], P('groups'), parts along dimension 0, may hold values from 0 to 319, as said below
- candidates: int32 [16, 32], P(('groups', 'pages')), parts along dimension 0, may hold values from 0 to 319, as said below
Outputs:
- scores: float32 [16, 32], P(('groups', 'pages')), parts along dimension 0
There are 2 independent parts, one for each index of `groups`. A program takes and returns all parts, laid end to end along the dimension named above; each array names one. Nothing has to cross between parts.
Inputs may be any that keep to these rules, and one draw needn't show every extreme that they name: A permutation: page id c is stored at row page_rows[c] of gallery, which lies on pages index page_rows[c] // 80. Each query's 32 page ids are distinct. The 2 queries of one pages index have at most 48 candidates stored on one pages index, and in every draw some pages index stores exactly 48 candidates of the queries of every pages index.
All inputs are finite; a program needn't handle non-finite values.
Results may differ from a plain program's by a relative error of at most 0.0003.
Values may be sent and summed in bfloat16 or wider, within the bound.
No kernel may reach another device: no remote copies, remote signals or barrier semaphores. Data moves between devices by JAX's collectives and lax.ppermute only.
A program may use at most 64 MiB of HBM per device.

v0:
```python
import functools

import jax
import jax.numpy as jnp
from jax import lax
from jax.experimental import pallas as pl
from jax.experimental.pallas import tpu as pltpu
from jax.sharding import PartitionSpec as P

LANES = 128
SUBLANES = 8
BASE = 128
INFO = 8
GROUP_PAGES = 16
UNROLLED = 3
LOADS = 4
GROUP = ("pages", "patches")
VMEM = pl.BlockSpec(memory_space=pltpu.VMEM)
HBM = pl.BlockSpec(memory_space=pltpu.HBM)


def sizes(queries, cand):
    count = queries * cand
    repeat = max(1, LANES // count)
    return count, repeat, count * repeat // LANES


def start_kernel(
    candidates_hbm, page_rows_hbm, tokens_hbm, gallery_hbm, info_ref, tokens_ref, first_ref, candidates_ref, page_rows_ref, sems
):
    copies = [
        pltpu.make_async_copy(page_rows_hbm, page_rows_ref, sems.at[0]),
        pltpu.make_async_copy(candidates_hbm, candidates_ref, sems.at[1]),
        pltpu.make_async_copy(tokens_hbm, tokens_ref, sems.at[2]),
        pltpu.make_async_copy(gallery_hbm.at[pl.ds(0, first_ref.shape[0])], first_ref, sems.at[3]),
    ]
    for copy in copies:
        copy.start()
    for copy in copies[:2]:
        copy.wait()
    queries, cand = candidates_ref.shape
    pages = page_rows_ref.shape[0]
    _, repeat, blocks = sizes(queries, cand)
    table = page_rows_ref[...].reshape(1, pages).astype(jnp.float32)
    high = jnp.floor(table * (1.0 / BASE))
    low = table - high * BASE
    digits = jnp.concatenate([high, low, jnp.zeros((6, pages), jnp.float32)], axis=0)
    found = []
    for q in range(queries):
        ids = candidates_ref[q : q + 1, :]
        hit = lax.broadcasted_iota(jnp.int32, (pages, cand), 0) == ids
        found.append(
            lax.dot_general(
                digits.astype(jnp.bfloat16),
                hit.astype(jnp.float32).astype(jnp.bfloat16),
                (((1,), (0,)), ((), ())),
                preferred_element_type=jnp.float32,
            )
        )
    line = jnp.concatenate(found * repeat, axis=1)
    rows = [line[0:1, r * LANES : (r + 1) * LANES] for r in range(blocks)]
    rows += [line[1:2, r * LANES : (r + 1) * LANES] for r in range(blocks)]
    if 2 * blocks < INFO:
        rows.append(jnp.zeros((INFO - 2 * blocks, LANES), jnp.float32))
    info_ref[...] = jnp.concatenate(rows, axis=0).astype(jnp.bfloat16)
    for copy in copies[2:]:
        copy.wait()


def in_hbm(x):
    return pltpu.with_memory_space_constraint(x, pltpu.HBM)


def start(candidates, page_rows, tokens, gallery, first):
    return pl.pallas_call(
        start_kernel,
        out_shape=(
            jax.ShapeDtypeStruct((INFO, LANES), jnp.bfloat16),
            jax.ShapeDtypeStruct(tokens.shape, tokens.dtype),
            jax.ShapeDtypeStruct((first, *gallery.shape[1:]), gallery.dtype),
        ),
        in_specs=[HBM] * 4,
        out_specs=(VMEM, VMEM, VMEM),
        scratch_shapes=[
            pltpu.VMEM(candidates.shape, jnp.int32),
            pltpu.VMEM(page_rows.shape, jnp.int32),
            pltpu.SemaphoreType.DMA((4,)),
        ],
        compiler_params=pltpu.CompilerParams(vmem_limit_bytes=8 << 20),
        cost_estimate=pl.CostEstimate(flops=1 << 20, transcendentals=0, bytes_accessed=1 << 20),
        name="start",
    )(in_hbm(candidates), in_hbm(page_rows), in_hbm(tokens), in_hbm(gallery))


def load_kernel(first, gallery_hbm, out_ref, sems):
    share = out_ref.shape[0] // LOADS
    copies = [
        pltpu.make_async_copy(
            gallery_hbm.at[pl.ds(first + i * share, share)], out_ref.at[pl.ds(i * share, share)], sems.at[i]
        )
        for i in range(LOADS)
    ]
    for copy in copies:
        copy.start()
    for copy in copies:
        copy.wait()


def load(gallery, first, count):
    shape = (count, *gallery.shape[1:])
    return pl.pallas_call(
        functools.partial(load_kernel, first),
        out_shape=jax.ShapeDtypeStruct(shape, gallery.dtype),
        in_specs=[HBM],
        out_specs=VMEM,
        scratch_shapes=[pltpu.SemaphoreType.DMA((LOADS,))],
        cost_estimate=pl.CostEstimate(
            flops=0, transcendentals=0, bytes_accessed=4 * count * gallery.shape[1] * gallery.shape[2]
        ),
        compiler_params=pltpu.CompilerParams(vmem_limit_bytes=8 << 20),
    )(in_hbm(gallery))


def arrange(order, shift, packed_refs, token_ref, columns):
    dim = packed_refs[0].shape[1]
    piece_rows = columns // len(order)
    held = columns // len(packed_refs)
    planes = 1 + max(plane for plane, _ in order)
    plane_rows = columns // planes
    here = lax.shift_right_logical(lax.axis_index("patches"), shift)
    double = token_ref.shape[1] // dim
    if double == 2:
        token_ref[:columns, dim:] = jnp.zeros((columns, dim), token_ref.dtype)
        token_ref[columns:, :dim] = jnp.zeros((columns, dim), token_ref.dtype)
    for i, (plane, flip) in enumerate(order):
        at = plane * plane_rows + jnp.bitwise_xor(here, flip) * piece_rows
        start = i * piece_rows % held
        piece = packed_refs[i * piece_rows // held][start : start + piece_rows, :]
        for k in range(double):
            rows = pl.ds(pl.multiple_of(at + k * columns, piece_rows), piece_rows)
            token_ref[rows, k * dim : (k + 1) * dim] = piece


def scan(gallery_ref, begin, token_ref, best_ref):
    pages, patches, dim = gallery_ref.shape
    columns = best_ref.shape[1]
    double = token_ref.shape[1] // dim
    width = min(columns, 256)
    share = GROUP_PAGES // double

    def step(i, carry):
        at = i * GROUP_PAGES
        if not isinstance(i, int):
            at = pl.multiple_of(at, GROUP_PAGES)
        sides = [gallery_ref[pl.ds(at + k * share, share)].reshape(share * patches, dim) for k in range(double)]
        patch = sides[0] if double == 1 else jnp.concatenate(sides, axis=1)
        for c in range(0, columns, width):
            sims = lax.dot_general(
                patch,
                token_ref[c : c + width * double, :],
                (((1,), (1,)), ((), ())),
                preferred_element_type=jnp.float32,
            )
            top = jnp.max(sims.reshape(share, patches, width * double), axis=1)
            for k in range(double):
                best_ref[pl.ds(begin + at + k * share, share), c : c + width] = top[:, k * width : (k + 1) * width]
        return carry

    steps = pages // GROUP_PAGES
    if double == 2 and steps <= UNROLLED:
        for i in range(steps):
            step(i, 0)
    else:
        lax.fori_loop(0, steps, step, 0)


def select(order, queries, cand, packed_refs, best_ref, out_ref):
    pages, columns = best_ref.shape
    info_start = columns // len(packed_refs)
    planes = 1 + max(plane for plane, _ in order)
    pieces = len(order) // planes
    plane_rows = columns // planes
    piece_rows = plane_rows // pieces
    each = piece_rows // queries
    count, repeat, blocks = sizes(queries, cand)
    held_tokens = each * pieces // repeat
    first = lax.axis_index("pages") * pages
    lane = lax.broadcasted_iota(jnp.int32, (1, LANES), 1)
    for d in range(planes):
        left = best_ref[:, d * plane_rows : (d + 1) * plane_rows]
        digits = []
        for _ in range(3):
            digits.append(left.astype(jnp.bfloat16))
            left = left - digits[-1].astype(jnp.float32)
        block = jnp.concatenate(digits, axis=0)
        info = packed_refs[0][info_start + d * INFO : info_start + (d + 1) * INFO, :].astype(jnp.float32)
        for r in range(blocks):
            rows = (info[r : r + 1, :] * BASE + info[blocks + r : blocks + r + 1, :]).astype(jnp.int32)
            local = rows - first
            held = (local >= 0) & (local < pages)
            pick = (lax.broadcasted_iota(jnp.int32, (pages, LANES), 0) == local).astype(jnp.float32)
            pick = pick.astype(jnp.bfloat16)
            got = lax.dot_general(
                block,
                jnp.concatenate([pick] * 3, axis=0),
                (((0,), (0,)), ((), ())),
                preferred_element_type=jnp.float32,
            )
            owner = ((r * LANES + lane) % count) // cand
            parts = []
            for i in range(pieces):
                at = i * piece_rows
                mine = got[at : at + each, :]
                for q in range(1, queries):
                    mine = jnp.where(owner == q, got[at + q * each : at + (q + 1) * each, :], mine)
                parts.append(mine)
            mine = jnp.where(held, jnp.concatenate(parts, axis=0), -jnp.inf)
            line = mine[0:held_tokens, :]
            for k in range(1, repeat):
                line = jnp.where(lane // count == k, mine[k * held_tokens : (k + 1) * held_tokens, :], line)
            out_ref[d, r] = line


def near_first_kernel(order, shift, count, *refs):
    packed_refs, (gallery_ref, best_ref, token_ref) = refs[:count], refs[count:]
    arrange(order, shift, packed_refs, token_ref, best_ref.shape[1])
    scan(gallery_ref, 0, token_ref, best_ref)


def near_second_kernel(queries, cand, order, shift, count, *refs):
    packed_refs, (first_ref, *gallery_refs, out_ref, token_ref, best_ref) = refs[:count], refs[count:]
    arrange(order, shift, packed_refs, token_ref, best_ref.shape[1])
    begin = 0
    for ref in gallery_refs:
        scan(ref, begin, token_ref, best_ref)
        begin += ref.shape[0]
    best_ref[begin : begin + first_ref.shape[0], :] = first_ref[...]
    select(order, queries, cand, packed_refs, best_ref, out_ref)


def far_kernel(queries, cand, order, shift, count, *refs):
    packed_refs, (*gallery_refs, out_ref, token_ref, best_ref) = refs[:count], refs[count:]
    arrange(order, shift, packed_refs, token_ref, best_ref.shape[1])
    begin = 0
    for ref in gallery_refs:
        scan(ref, begin, token_ref, best_ref)
        begin += ref.shape[0]
    select(order, queries, cand, packed_refs, best_ref, out_ref)


def finish_kernel(queries, cand, tokens, mine_ref, other_ref, scores_ref):
    count, repeat, blocks = sizes(queries, cand)
    lines = []
    for r in range(blocks):
        best = jnp.maximum(mine_ref[r], other_ref[r])
        total = jnp.sum(best, axis=0, keepdims=True)
        line = total[:, : LANES // repeat]
        for k in range(1, repeat):
            line = line + total[:, k * count : (k + 1) * count]
        lines.append(line)
    line = lines[0] if blocks == 1 else jnp.concatenate(lines, axis=1)
    for q in range(queries):
        scores_ref[q : q + 1, :] = line[:, q * cand : (q + 1) * cand] * (1.0 / tokens)


def body(queries, gallery, page_rows, candidates):
    planes = lax.axis_size("pages")
    parts = lax.axis_size("patches")
    everyone = planes * parts
    query_count, own_tokens, dim = queries.shape
    tokens = own_tokens * parts
    cand = candidates.shape[1]
    _, repeat, blocks = sizes(query_count, cand)
    pages, patches, _ = gallery.shape

    def swap(x, mask):
        return lax.ppermute(x, GROUP, [(i, i ^ mask) for i in range(everyone)])

    def mask_of(bit):
        return bit if bit == 1 else bit | 1

    last = GROUP_PAGES * max(1, pages // GROUP_PAGES // 5)
    first = GROUP_PAGES * ((pages - last) // GROUP_PAGES // 2)
    middle = pages - first - last
    info, own, gallery_a = start(candidates, page_rows, queries, gallery, first)
    gallery_b = load(gallery, first, middle)
    gallery_c = load(gallery, first + middle, last)
    held, bit, shift = queries, 1, 0
    while held.shape[1] % SUBLANES and bit < parts:
        other = swap(held, mask_of(bit))
        upper = (lax.axis_index("patches") & bit) != 0
        held = jnp.concatenate([jnp.where(upper, other, held), jnp.where(upper, held, other)], axis=1)
        bit, shift = bit * 2, shift + 1
    pieces = held.reshape(-1, dim)
    order = [(0, 0)]

    def double_up(pieces, order, mask):
        other = swap(pieces, mask)
        mine = own.reshape(pieces.shape) if len(order) == 1 and not shift else pieces
        return jnp.concatenate([mine, other], axis=0), order + [(p, (mask % parts >> shift) ^ f) for p, f in order]

    for bit in [1 << k for k in range(max(1, shift), parts.bit_length() - 1)]:
        pieces, order = double_up(pieces, order, mask_of(bit))
    infos = info
    hops = [1 << k for k in reversed(range(planes.bit_length() - 1))]
    for bit in hops[:-1]:
        mask = (bit * parts) | 1
        known = infos.shape[0] // INFO
        split = pieces.shape[0]
        other = swap(jnp.concatenate([pieces, infos], axis=0), mask)
        pieces = jnp.concatenate([pieces, other[:split]], axis=0)
        infos = jnp.concatenate([infos, other[split:]], axis=0)
        order = order + [(p + known, (mask % parts >> shift) ^ f) for p, f in order]
    mask = (hops[-1] * parts) | 1
    split = pieces.shape[0]
    sent = jnp.concatenate([pieces, infos], axis=0)
    other = swap(sent, mask)
    packed, other = [sent], [other]
    flips = [(p, (mask % parts >> shift) ^ f) for p, f in order]
    if not shift:
        packed.append(swap(pieces, 1))
        other.append(swap(other[0][:split], 1))
        order = order + [(p, 1 ^ f) for p, f in order]
        flips = flips + [(p, 1 ^ f) for p, f in flips]

    columns = planes // 2 * query_count * tokens
    double = 2 if columns <= 128 else 1
    token_scratch = pltpu.VMEM((columns * double, dim * double), jnp.bfloat16)
    best_scratch = pltpu.VMEM((pages, columns), jnp.float32)
    message = jax.ShapeDtypeStruct((planes // 2, blocks, tokens // repeat, LANES), jnp.float32)

    def call(kernel, count, **kwargs):
        return pl.pallas_call(
            kernel,
            cost_estimate=pl.CostEstimate(
                flops=2 * count * patches * dim * columns, transcendentals=0, bytes_accessed=count * patches * dim * 2
            ),
            compiler_params=pltpu.CompilerParams(vmem_limit_bytes=24 << 20),
            **kwargs,
        )

    near_best = call(
        functools.partial(near_first_kernel, order, shift, len(packed)),
        last,
        out_shape=jax.ShapeDtypeStruct((last, columns), jnp.float32),
        in_specs=[VMEM] * (len(packed) + 1),
        out_specs=VMEM,
        scratch_shapes=[token_scratch],
    )(*packed, gallery_c)
    far = call(
        functools.partial(far_kernel, query_count, cand, flips, shift, len(other)),
        pages,
        out_shape=message,
        in_specs=[VMEM] * (len(packed) + 3),
        out_specs=VMEM,
        scratch_shapes=[token_scratch, best_scratch],
    )(*other, gallery_a, gallery_b, gallery_c)
    near = call(
        functools.partial(near_second_kernel, query_count, cand, order, shift, len(packed)),
        pages - last,
        out_shape=message,
        in_specs=[VMEM] * (len(packed) + 3),
        out_specs=VMEM,
        scratch_shapes=[token_scratch, best_scratch],
    )(*packed, near_best, gallery_a, gallery_b)
    for bit in reversed(hops):
        arrived = swap(far, (bit * parts) | 1)
        best = jnp.maximum(near, arrived)
        half = best.shape[0] // 2
        near, far = best[:half], best[half:]
    best = best[0]
    bit = parts // 2
    while bit > 1:
        best = jnp.maximum(best, swap(best, mask_of(bit)))
        bit //= 2
    return pl.pallas_call(
        functools.partial(finish_kernel, query_count, cand, tokens),
        out_shape=jax.ShapeDtypeStruct((query_count, cand), jnp.float32),
        in_specs=[VMEM, VMEM],
        out_specs=VMEM,
        compiler_params=pltpu.CompilerParams(vmem_limit_bytes=8 << 20),
        name="finish",
    )(best, swap(best, 1))


def solution(mesh):
    in_specs = (
        P(("groups", "pages"), "patches", None),
        P(("groups", "pages"), "patches", None),
        P("groups"),
        P(("groups", "pages"), None),
    )
    out_specs = P(("groups", "pages"), None)
    return jax.shard_map(body, mesh=mesh, in_specs=in_specs, out_specs=out_specs, check_vma=False)
```

profile of v0, /device:TPU:0, one launch (start us, length us, event | category | flops | bytes accessed | tf_op | source)
XLA Modules:
  0.0 29.6 jit_solution(9651454865752779757)
XLA Ops:
  0.0 2.4 %collective-permute-start = (bf16[16,128]{1,0:T(8,128)(2,1)}, bf16[16,128]{1,0:T(8,128)(2,1)S(1)}, u32[]{:S(2)}, u32[]{:S(2)}) collective-permute-start(bf16[16,128]{1,0:T(8,128)(2,1)} %bitcast.7), channel_id=1, source_target_pairs={{0,3},{1,2},{2,1},{3,0},{4,7},{5,6},{6,5},{7,4},{8,11},{9,10},{10,... | collective-permute-start | bytes 12296 | tf_op jit(solution)/shard_map/ppermute | solution.py:277
  2.4 1.7 %start.1 = (bf16[8,128]{1,0:T(8,128)(2,1)S(1)}, bf16[2,8,128]{2,1,0:T(8,128)(2,1)S(1)}, bf16[32,256,128]{2,1,0:T(8,128)(2,1)S(1)}) custom-call(s32[2,32]{1,0:T(2,128)} %candidates_hbm.1, s32[320]{0:T(512)} %page_rows_hbm.1, bf16[2,8,128]{2,1,0:T(8,128)(2,1)} %tokens_hbm.1, bf16[80,256,128]{2,1,0:T(8,128)(2,1)} %gallery_hbm.5), custom_call_target="tpu_custom_call" | custom-call | flops 1048576 | bytes 1048576 | tf_op jit(solution)/shard_map/start/pallas_call | solution.py:75
  4.1 0.0 collective-permute-done
  4.1 2.9 %collective-permute-start.1 = (bf16[40,128]{1,0:T(8,128)(2,1)S(1)}, bf16[40,128]{1,0:T(8,128)(2,1)S(1)}, u32[]{:S(2)}, u32[]{:S(2)}) collective-permute-start(bf16[40,128]{1,0:T(8,128)(2,1)S(1)} %pad_maximum_fusion.1), channel_id=1, source_target_pairs={{0,9},{1,8},{2,11},{3,10},{4,13},{5,12},{6,15},{7,14},{8,1},{9,0},... | collective-permute-start | bytes 30728 | tf_op jit(solution)/shard_map/ppermute | solution.py:277
  7.1 1.4 %collective-permute-done.1 = bf16[40,128]{1,0:T(8,128)(2,1)S(1)} collective-permute-done((bf16[40,128]{1,0:T(8,128)(2,1)S(1)}, bf16[40,128]{1,0:T(8,128)(2,1)S(1)}, u32[]{:S(2)}, u32[]{:S(2)}) %collective-permute-start.1) | collective-permute-done | bytes 10272 | tf_op jit(solution)/shard_map/ppermute | solution.py:277
  8.5 1.7 %collective-permute-start.3 = (bf16[80,128]{1,0:T(8,128)(2,1)S(1)}, bf16[80,128]{1,0:T(8,128)(2,1)S(1)}, u32[]{:S(2)}, u32[]{:S(2)}) collective-permute-start(bf16[80,128]{1,0:T(8,128)(2,1)S(1)} %constant_dynamic-update-slice_fusion.refs_0_), channel_id=1, source_target_pairs={{0,5},{1,4},{2,7},{3,6},{4,1},{5,0},{6,3},{7,2},{8,13},{9,12},{10,... | collective-permute-start | bytes 61448 | tf_op jit(solution)/shard_map/ppermute | solution.py:277
  10.1 0.4 %collective-permute-start.2 = (bf16[64,128]{1,0:T(8,128)(2,1)S(1)}, bf16[64,128]{1,0:T(8,128)(2,1)S(1)}, u32[]{:S(2)}, u32[]{:S(2)}) collective-permute-start(bf16[64,128]{1,0:T(8,128)(2,1)S(1)} %pad_maximum_fusion), channel_id=1, source_target_pairs={{0,1},{1,0},{2,3},{3,2},{4,5},{5,4},{6,7},{7,6},{8,9},{9,8},{10,11... | collective-permute-start | bytes 49160 | tf_op jit(solution)/shard_map/ppermute | solution.py:277
  10.5 1.2 %collective-permute-done.3.refs_0_ = bf16[80,128]{1,0:T(8,128)(2,1)S(1)} collective-permute-done((bf16[80,128]{1,0:T(8,128)(2,1)S(1)}, bf16[80,128]{1,0:T(8,128)(2,1)S(1)}, u32[]{:S(2)}, u32[]{:S(2)}) %collective-permute-start.3) | collective-permute-done | bytes 20512 | tf_op jit(solution)/shard_map/ppermute | solution.py:277
  11.7 0.4 %collective-permute-start.4 = (bf16[64,128]{1,0:T(8,128)(2,1)S(1)}, bf16[64,128]{1,0:T(8,128)(2,1)S(1)}, u32[]{:S(2)}, u32[]{:S(2)}) collective-permute-start(bf16[64,128]{1,0:T(8,128)(2,1)S(1)} %slice.22), channel_id=1, source_target_pairs={{0,1},{1,0},{2,3},{3,2},{4,5},{5,4},{6,7},{7,6},{8,9},{9,8},{10,11... | collective-permute-start | bytes 49160 | tf_op jit(solution)/shard_map/ppermute | solution.py:277
  12.2 1.2 %shard_map.46.refs_2_.refs_4_ = bf16[16,256,128]{2,1,0:T(8,128)(2,1)S(1)} custom-call(bf16[80,256,128]{2,1,0:T(8,128)(2,1)} %gallery_hbm.5), custom_call_target="tpu_custom_call" | custom-call | bytes 2097152 | tf_op jit(solution)/shard_map/pallas_call | solution.py:111
  13.4 1.6 %shard_map.48.refs_4_.refs_3_ = bf16[32,256,128]{2,1,0:T(8,128)(2,1)S(1)} custom-call(bf16[80,256,128]{2,1,0:T(8,128)(2,1)} %gallery_hbm.5), custom_call_target="tpu_custom_call" | custom-call | bytes 4194304 | tf_op jit(solution)/shard_map/pallas_call | solution.py:111
  14.9 0.0 collective-permute-done.2.refs_1_
  15.0 0.5 %shard_map.47.refs_2_ = f32[16,128]{1,0:T(8,128)S(1)} custom-call(bf16[80,128]{1,0:T(8,128)(2,1)S(1)} %constant_dynamic-update-slice_fusion.refs_0_, bf16[64,128]{1,0:T(8,128)(2,1)S(1)} %collective-permute-done.2.refs_1_, bf16[16,256,128]{2,1,0:T(8,128)(2,1)S(1)} %shard_map.46.refs_2_.refs_4_), custom_call_target="tpu_custom_call" | custom-call | flops 134217728 | bytes 1048576 | tf_op jit(solution)/shard_map/pallas_call | solution.py:342
  15.5 0.0 collective-permute-done.4.refs_1_
  15.5 1.9 %shard_map.50 = f32[2,1,16,128]{3,2,1,0:T(8,128)S(1)} custom-call(bf16[80,128]{1,0:T(8,128)(2,1)S(1)} %collective-permute-done.3.refs_0_, bf16[64,128]{1,0:T(8,128)(2,1)S(1)} %collective-permute-done.4.refs_1_, bf16[32,256,128]{2,1,0:T(8,128)(2,1)S(1)} %get-tuple-element.10.refs_3_.refs_2_, bf16[32,256,128]{2,1,0:T(8,128)(2,1)S(1)} %shard_map.48.refs_4_.refs_3_, ...), custom_call_target="tpu_custom_call" | custom-call | flops 671088640 | bytes 5242880 | tf_op jit(solution)/shard_map/pallas_call | solution.py:350
  17.4 1.6 %collective-permute-start.5 = (f32[2,1,16,128]{3,2,1,0:T(8,128)S(1)}, f32[2,1,16,128]{3,2,1,0:T(8,128)S(1)}, u32[]{:S(2)}, u32[]{:S(2)}) collective-permute-start(f32[2,1,16,128]{3,2,1,0:T(8,128)S(1)} %shard_map.50), channel_id=1, source_target_pairs={{0,5},{1,4},{2,7},{3,6},{4,1},{5,0},{6,3},{7,2},{8,13},{9,12},{10,... | collective-permute-start | bytes 49160 | tf_op jit(solution)/shard_map/ppermute | solution.py:277
  19.0 1.6 %shard_map.49 = f32[2,1,16,128]{3,2,1,0:T(8,128)S(1)} custom-call(bf16[80,128]{1,0:T(8,128)(2,1)S(1)} %constant_dynamic-update-slice_fusion.refs_0_, bf16[64,128]{1,0:T(8,128)(2,1)S(1)} %collective-permute-done.2.refs_1_, f32[16,128]{1,0:T(8,128)S(1)} %shard_map.47.refs_2_, bf16[32,256,128]{2,1,0:T(8,128)(2,1)S(1)} %get-tuple-element.10.refs_3_.refs_2_, ...), custom_call_target="tpu_custom_call" | custom-call | flops 536870912 | bytes 4194304 | tf_op jit(solution)/shard_map/pallas_call | solution.py:358
  20.6 0.0 collective-permute-done.5
  20.6 2.5 %collective-permute-start.6 = (f32[1,1,16,128]{3,2,1,0:T(8,128)S(1)}, f32[1,1,16,128]{3,2,1,0:T(8,128)S(1)}, u32[]{:S(2)}, u32[]{:S(2)}) collective-permute-start(f32[1,1,16,128]{3,2,1,0:T(8,128)S(1)} %slice.24), channel_id=1, source_target_pairs={{0,9},{1,8},{2,11},{3,10},{4,13},{5,12},{6,15},{7,14},{8,1},{9,0},... | collective-permute-start | bytes 24584 | tf_op jit(solution)/shard_map/ppermute | solution.py:277
  23.2 1.5 %collective-permute-done.6 = f32[1,1,16,128]{3,2,1,0:T(8,128)S(1)} collective-permute-done((f32[1,1,16,128]{3,2,1,0:T(8,128)S(1)}, f32[1,1,16,128]{3,2,1,0:T(8,128)S(1)}, u32[]{:S(2)}, u32[]{:S(2)}) %collective-permute-start.6) | collective-permute-done | bytes 8224 | tf_op jit(solution)/shard_map/ppermute | solution.py:277
  24.7 1.4 %collective-permute-start.7 = (f32[1,16,128]{2,1,0:T(8,128)S(1)}, f32[1,16,128]{2,1,0:T(8,128)S(1)}, u32[]{:S(2)}, u32[]{:S(2)}) collective-permute-start(f32[1,16,128]{2,1,0:T(8,128)S(1)} %fusion), channel_id=1, source_target_pairs={{0,3},{1,2},{2,1},{3,0},{4,7},{5,6},{6,5},{7,4},{8,11},{9,10},{10,... | collective-permute-start | bytes 24584 | tf_op jit(solution)/shard_map/ppermute | solution.py:277
  26.1 1.7 %collective-permute-done.7 = f32[1,16,128]{2,1,0:T(8,128)S(1)} collective-permute-done((f32[1,16,128]{2,1,0:T(8,128)S(1)}, f32[1,16,128]{2,1,0:T(8,128)S(1)}, u32[]{:S(2)}, u32[]{:S(2)}) %collective-permute-start.7) | collective-permute-done | bytes 8224 | tf_op jit(solution)/shard_map/ppermute | solution.py:277
  27.7 0.1 collective-permute-start.8
  27.9 1.0 %collective-permute-done.8.other_ref = f32[1,16,128]{2,1,0:T(8,128)S(1)} collective-permute-done((f32[1,16,128]{2,1,0:T(8,128)S(1)}, f32[1,16,128]{2,1,0:T(8,128)S(1)}, u32[]{:S(2)}, u32[]{:S(2)}) %collective-permute-start.8) | collective-permute-done | bytes 8224 | tf_op jit(solution)/shard_map/ppermute | solution.py:277
  28.9 0.7 %finish.1 = f32[2,32]{1,0:T(2,128)} custom-call(f32[1,16,128]{2,1,0:T(8,128)S(1)} %max.11.mine_ref, f32[1,16,128]{2,1,0:T(8,128)S(1)} %collective-permute-done.8.other_ref), custom_call_target="tpu_custom_call" | custom-call | tf_op jit(solution)/shard_map/finish/pallas_call | solution.py:376
  (12 shorter events, 0.1 us)
Async XLA Ops:
  0.0 4.1 %collective-permute-start = (bf16[16,128]{1,0:T(8,128)(2,1)}, bf16[16,128]{1,0:T(8,128)(2,1)S(1)}, u32[]{:S(2)}, u32[]{:S(2)}) collective-permute-start(bf16[16,128]{1,0:T(8,128)(2,1)} %bitcast.7), channel_id=1, source_target_pairs={{0,3},{1,2},{2,1},{3,0},{4,7},{5,6},{6,5},{7,4},{8,11},{9,10},{10,... | collective-permute-start | bytes 12296 | tf_op jit(solution)/shard_map/ppermute | solution.py:277
  4.1 4.3 %collective-permute-start.1 = (bf16[40,128]{1,0:T(8,128)(2,1)S(1)}, bf16[40,128]{1,0:T(8,128)(2,1)S(1)}, u32[]{:S(2)}, u32[]{:S(2)}) collective-permute-start(bf16[40,128]{1,0:T(8,128)(2,1)S(1)} %pad_maximum_fusion.1), channel_id=1, source_target_pairs={{0,9},{1,8},{2,11},{3,10},{4,13},{5,12},{6,15},{7,14},{8,1},{9,0},... | collective-permute-start | bytes 30728 | tf_op jit(solution)/shard_map/ppermute | solution.py:277
  8.5 3.3 %collective-permute-start.3 = (bf16[80,128]{1,0:T(8,128)(2,1)S(1)}, bf16[80,128]{1,0:T(8,128)(2,1)S(1)}, u32[]{:S(2)}, u32[]{:S(2)}) collective-permute-start(bf16[80,128]{1,0:T(8,128)(2,1)S(1)} %constant_dynamic-update-slice_fusion.refs_0_), channel_id=1, source_target_pairs={{0,5},{1,4},{2,7},{3,6},{4,1},{5,0},{6,3},{7,2},{8,13},{9,12},{10,... | collective-permute-start | bytes 61448 | tf_op jit(solution)/shard_map/ppermute | solution.py:277
  10.1 4.8 %collective-permute-start.2 = (bf16[64,128]{1,0:T(8,128)(2,1)S(1)}, bf16[64,128]{1,0:T(8,128)(2,1)S(1)}, u32[]{:S(2)}, u32[]{:S(2)}) collective-permute-start(bf16[64,128]{1,0:T(8,128)(2,1)S(1)} %pad_maximum_fusion), channel_id=1, source_target_pairs={{0,1},{1,0},{2,3},{3,2},{4,5},{5,4},{6,7},{7,6},{8,9},{9,8},{10,11... | collective-permute-start | bytes 49160 | tf_op jit(solution)/shard_map/ppermute | solution.py:277
  11.7 3.7 %collective-permute-start.4 = (bf16[64,128]{1,0:T(8,128)(2,1)S(1)}, bf16[64,128]{1,0:T(8,128)(2,1)S(1)}, u32[]{:S(2)}, u32[]{:S(2)}) collective-permute-start(bf16[64,128]{1,0:T(8,128)(2,1)S(1)} %slice.22), channel_id=1, source_target_pairs={{0,1},{1,0},{2,3},{3,2},{4,5},{5,4},{6,7},{7,6},{8,9},{9,8},{10,11... | collective-permute-start | bytes 49160 | tf_op jit(solution)/shard_map/ppermute | solution.py:277
  17.4 3.2 %collective-permute-start.5 = (f32[2,1,16,128]{3,2,1,0:T(8,128)S(1)}, f32[2,1,16,128]{3,2,1,0:T(8,128)S(1)}, u32[]{:S(2)}, u32[]{:S(2)}) collective-permute-start(f32[2,1,16,128]{3,2,1,0:T(8,128)S(1)} %shard_map.50), channel_id=1, source_target_pairs={{0,5},{1,4},{2,7},{3,6},{4,1},{5,0},{6,3},{7,2},{8,13},{9,12},{10,... | collective-permute-start | bytes 49160 | tf_op jit(solution)/shard_map/ppermute | solution.py:277
  20.6 4.0 %collective-permute-start.6 = (f32[1,1,16,128]{3,2,1,0:T(8,128)S(1)}, f32[1,1,16,128]{3,2,1,0:T(8,128)S(1)}, u32[]{:S(2)}, u32[]{:S(2)}) collective-permute-start(f32[1,1,16,128]{3,2,1,0:T(8,128)S(1)} %slice.24), channel_id=1, source_target_pairs={{0,9},{1,8},{2,11},{3,10},{4,13},{5,12},{6,15},{7,14},{8,1},{9,0},... | collective-permute-start | bytes 24584 | tf_op jit(solution)/shard_map/ppermute | solution.py:277
  24.7 3.1 %collective-permute-start.7 = (f32[1,16,128]{2,1,0:T(8,128)S(1)}, f32[1,16,128]{2,1,0:T(8,128)S(1)}, u32[]{:S(2)}, u32[]{:S(2)}) collective-permute-start(f32[1,16,128]{2,1,0:T(8,128)S(1)} %fusion), channel_id=1, source_target_pairs={{0,3},{1,2},{2,1},{3,0},{4,7},{5,6},{6,5},{7,4},{8,11},{9,10},{10,... | collective-permute-start | bytes 24584 | tf_op jit(solution)/shard_map/ppermute | solution.py:277
  27.7 1.2 %collective-permute-start.8 = (f32[1,16,128]{2,1,0:T(8,128)S(1)}, f32[1,16,128]{2,1,0:T(8,128)S(1)}, u32[]{:S(2)}, u32[]{:S(2)}) collective-permute-start(f32[1,16,128]{2,1,0:T(8,128)S(1)} %max.11.mine_ref), channel_id=1, source_target_pairs={{0,1},{1,0},{2,3},{3,2},{4,5},{5,4},{6,7},{7,6},{8,9},{9,8},{10,11... | collective-permute-start | bytes 24584 | tf_op jit(solution)/shard_map/ppermute | solution.py:277
where the time goes:
time: 29.8 us; the launch traced here: 29.6 us
  starting transfers between devices  13.5 us (45%)
  Pallas kernels  9.11 us (31%)
  waiting for transfers between devices  6.82 us (23%)
    ppermute x9, starting transfers between devices, swap(): return lax.ppermute(x, GROUP, [(i, i ^ mask) for i in range(everyone)])  13.5 us
    ppermute x9, waiting for transfers between devices, swap(): return lax.ppermute(x, GROUP, [(i, i ^ mask) for i in range(everyone)])  6.82 us
    pallas_call x2, Pallas kernels, load(): pl.pallas_call(functools.partial(load_kernel, first), out_shape=jax.Shape...  2.77 us
    pallas_call x1, Pallas kernels, body(): call(functools.partial(far_kernel, query_count, cand, flips, shift, len(o...  1.88 us
    pallas_call x1, Pallas kernels, start(): pl.pallas_call(start_kernel, out_shape=(jax.ShapeDtypeStruct((INFO, LANES...  1.67 us
    pallas_call x1, Pallas kernels, body(): call(functools.partial(near_second_kernel, query_count, cand, order, shif...  1.58 us
    pallas_call x1, Pallas kernels, body(): pl.pallas_call(functools.partial(finish_kernel, query_count, cand, tokens...  0.71 us
  transfers between devices with their start and end apart: 9, of which 5 were waited for; matrix products, arithmetic and copies ran while one was open for 0% of the time, Pallas kernels for 22%

commit v1 on v0

--- a/solution.py
+++ b/solution.py
@@ -130,8 +130,7 @@
     here = lax.shift_right_logical(lax.axis_index("patches"), shift)
     double = token_ref.shape[1] // dim
     if double == 2:
-        token_ref[:columns, dim:] = jnp.zeros((columns, dim), token_ref.dtype)
-        token_ref[columns:, :dim] = jnp.zeros((columns, dim), token_ref.dtype)
+        token_ref[...] = jnp.zeros_like(token_ref)
     for i, (plane, flip) in enumerate(order):
         at = plane * plane_rows + jnp.bitwise_xor(here, flip) * piece_rows
         start = i * piece_rows % held
@@ -280,7 +279,7 @@
         return bit if bit == 1 else bit | 1
 
     last = GROUP_PAGES * max(1, pages // GROUP_PAGES // 5)
-    first = GROUP_PAGES * ((pages - last) // GROUP_PAGES // 2)
+    first = GROUP_PAGES * ((pages - last) // GROUP_PAGES * 3 // 4)
     middle = pages - first - last
     info, own, gallery_a = start(candidates, page_rows, queries, gallery, first)
     gallery_b = load(gallery, first, middle)

time: 29.8 us -> 29.7 us (level)
  starting transfers between devices: 13.5 us -> 12.6 us
  waiting for transfers between devices: 6.82 us -> 7.68 us
    ppermute x9, starting transfers between devices: 13.5 us -> 12.6 us  [swap(): return lax.ppermute(x, GROUP, [(i, i ^ mask) for i in range(everyone)])]
    ppermute x9, waiting for transfers between devices: 6.82 us -> 7.68 us  [swap(): return lax.ppermute(x, GROUP, [(i, i ^ mask) for i in range(everyone)])]
    pallas_call x2, Pallas kernels: 2.77 us -> 2.44 us  [load(): pl.pallas_call(functools.partial(load_kernel, first), out_shape=jax.Shape...]
    pallas_call x1, Pallas kernels: 1.67 us -> 1.97 us  [start(): pl.pallas_call(start_kernel, out_shape=(jax.ShapeDtypeStruct((INFO, LANES...]
  transfers between devices with their start and end apart: 9 -> 9, of which waited for: 5 -> 6; matrix products, arithmetic and copies ran while one was open for 0% -> 0% of each run, Pallas kernels for 22% -> 22%
where the time goes in v1:
time: 29.7 us; the launch traced here: 29.5 us
  starting transfers between devices  12.6 us (42%)
  Pallas kernels  9.09 us (31%)
  waiting for transfers between devices  7.68 us (26%)
    ppermute x9, starting transfers between devices, swap(): return lax.ppermute(x, GROUP, [(i, i ^ mask) for i in range(everyone)])  12.6 us
    ppermute x9, waiting for transfers between devices, swap(): return lax.ppermute(x, GROUP, [(i, i ^ mask) for i in range(everyone)])  7.68 us
    pallas_call x2, Pallas kernels, load(): pl.pallas_call(functools.partial(load_kernel, first), out_shape=jax.Shape...  2.44 us
    pallas_call x1, Pallas kernels, start(): pl.pallas_call(start_kernel, out_shape=(jax.ShapeDtypeStruct((INFO, LANES...  1.97 us
    pallas_call x1, Pallas kernels, body(): call(functools.partial(far_kernel, query_count, cand, flips, shift, len(o...  1.88 us
    pallas_call x1, Pallas kernels, body(): call(functools.partial(near_second_kernel, query_count, cand, order, shif...  1.58 us
    pallas_call x1, Pallas kernels, body(): pl.pallas_call(functools.partial(finish_kernel, query_count, cand, tokens...  0.71 us
  transfers between devices with their start and end apart: 9, of which 6 were waited for; matrix products, arithmetic and copies ran while one was open for 0% of the time, Pallas kernels for 22%

profile of v1, /device:TPU:0, one launch (start us, length us, event | category | flops | bytes accessed | tf_op | source)
XLA Modules:
  0.0 29.5 jit_solution(7128013460948696069)
XLA Ops:
  0.0 2.4 %collective-permute-start = (bf16[16,128]{1,0:T(8,128)(2,1)}, bf16[16,128]{1,0:T(8,128)(2,1)S(1)}, u32[]{:S(2)}, u32[]{:S(2)}) collective-permute-start(bf16[16,128]{1,0:T(8,128)(2,1)} %bitcast.7), channel_id=1, source_target_pairs={{0,3},{1,2},{2,1},{3,0},{4,7},{5,6},{6,5},{7,4},{8,11},{9,10},{10,... | collective-permute-start | bytes 12296 | tf_op jit(solution)/shard_map/ppermute | solution.py:276
  2.4 2.0 %start.1 = (bf16[8,128]{1,0:T(8,128)(2,1)S(1)}, bf16[2,8,128]{2,1,0:T(8,128)(2,1)S(1)}, bf16[48,256,128]{2,1,0:T(8,128)(2,1)S(1)}) custom-call(s32[2,32]{1,0:T(2,128)} %candidates_hbm.1, s32[320]{0:T(512)} %page_rows_hbm.1, bf16[2,8,128]{2,1,0:T(8,128)(2,1)} %tokens_hbm.1, bf16[80,256,128]{2,1,0:T(8,128)(2,1)} %gallery_hbm.5), custom_call_target="tpu_custom_call" | custom-call | flops 1048576 | bytes 1048576 | tf_op jit(solution)/shard_map/start/pallas_call | solution.py:75
  4.4 0.0 collective-permute-done
  4.4 2.9 %collective-permute-start.1 = (bf16[40,128]{1,0:T(8,128)(2,1)S(1)}, bf16[40,128]{1,0:T(8,128)(2,1)S(1)}, u32[]{:S(2)}, u32[]{:S(2)}) collective-permute-start(bf16[40,128]{1,0:T(8,128)(2,1)S(1)} %pad_maximum_fusion.1), channel_id=1, source_target_pairs={{0,9},{1,8},{2,11},{3,10},{4,13},{5,12},{6,15},{7,14},{8,1},{9,0},... | collective-permute-start | bytes 30728 | tf_op jit(solution)/shard_map/ppermute | solution.py:276
  7.4 1.4 %collective-permute-done.1 = bf16[40,128]{1,0:T(8,128)(2,1)S(1)} collective-permute-done((bf16[40,128]{1,0:T(8,128)(2,1)S(1)}, bf16[40,128]{1,0:T(8,128)(2,1)S(1)}, u32[]{:S(2)}, u32[]{:S(2)}) %collective-permute-start.1) | collective-permute-done | bytes 10272 | tf_op jit(solution)/shard_map/ppermute | solution.py:276
  8.8 1.7 %collective-permute-start.3 = (bf16[80,128]{1,0:T(8,128)(2,1)S(1)}, bf16[80,128]{1,0:T(8,128)(2,1)S(1)}, u32[]{:S(2)}, u32[]{:S(2)}) collective-permute-start(bf16[80,128]{1,0:T(8,128)(2,1)S(1)} %constant_dynamic-update-slice_fusion.refs_0_), channel_id=1, source_target_pairs={{0,5},{1,4},{2,7},{3,6},{4,1},{5,0},{6,3},{7,2},{8,13},{9,12},{10,... | collective-permute-start | bytes 61448 | tf_op jit(solution)/shard_map/ppermute | solution.py:276
  10.4 0.1 collective-permute-start.2
  10.5 1.5 %collective-permute-done.3.refs_0_ = bf16[80,128]{1,0:T(8,128)(2,1)S(1)} collective-permute-done((bf16[80,128]{1,0:T(8,128)(2,1)S(1)}, bf16[80,128]{1,0:T(8,128)(2,1)S(1)}, u32[]{:S(2)}, u32[]{:S(2)}) %collective-permute-start.3) | collective-permute-done | bytes 20512 | tf_op jit(solution)/shard_map/ppermute | solution.py:276
  12.0 0.4 %collective-permute-start.4 = (bf16[64,128]{1,0:T(8,128)(2,1)S(1)}, bf16[64,128]{1,0:T(8,128)(2,1)S(1)}, u32[]{:S(2)}, u32[]{:S(2)}) collective-permute-start(bf16[64,128]{1,0:T(8,128)(2,1)S(1)} %slice.22), channel_id=1, source_target_pairs={{0,1},{1,0},{2,3},{3,2},{4,5},{5,4},{6,7},{7,6},{8,9},{9,8},{10,11... | collective-permute-start | bytes 49160 | tf_op jit(solution)/shard_map/ppermute | solution.py:276
  12.5 1.2 %shard_map.48.refs_4_.refs_3_ = bf16[16,256,128]{2,1,0:T(8,128)(2,1)S(1)} custom-call(bf16[80,256,128]{2,1,0:T(8,128)(2,1)} %gallery_hbm.5), custom_call_target="tpu_custom_call" | custom-call | bytes 2097152 | tf_op jit(solution)/shard_map/pallas_call | solution.py:111
  13.7 1.2 %shard_map.46.refs_2_.refs_4_ = bf16[16,256,128]{2,1,0:T(8,128)(2,1)S(1)} custom-call(bf16[80,256,128]{2,1,0:T(8,128)(2,1)} %gallery_hbm.5), custom_call_target="tpu_custom_call" | custom-call | bytes 2097152 | tf_op jit(solution)/shard_map/pallas_call | solution.py:111
  14.9 0.0 collective-permute-done.2.refs_1_
  14.9 0.5 %shard_map.47.refs_2_ = f32[16,128]{1,0:T(8,128)S(1)} custom-call(bf16[80,128]{1,0:T(8,128)(2,1)S(1)} %constant_dynamic-update-slice_fusion.refs_0_, bf16[64,128]{1,0:T(8,128)(2,1)S(1)} %collective-permute-done.2.refs_1_, bf16[16,256,128]{2,1,0:T(8,128)(2,1)S(1)} %shard_map.46.refs_2_.refs_4_), custom_call_target="tpu_custom_call" | custom-call | flops 134217728 | bytes 1048576 | tf_op jit(solution)/shard_map/pallas_call | solution.py:341
  15.4 0.0 collective-permute-done.4.refs_1_
  15.5 1.9 %shard_map.50 = f32[2,1,16,128]{3,2,1,0:T(8,128)S(1)} custom-call(bf16[80,128]{1,0:T(8,128)(2,1)S(1)} %collective-permute-done.3.refs_0_, bf16[64,128]{1,0:T(8,128)(2,1)S(1)} %collective-permute-done.4.refs_1_, bf16[48,256,128]{2,1,0:T(8,128)(2,1)S(1)} %get-tuple-element.10.refs_3_.refs_2_, bf16[16,256,128]{2,1,0:T(8,128)(2,1)S(1)} %shard_map.48.refs_4_.refs_3_, ...), custom_call_target="tpu_custom_call" | custom-call | flops 671088640 | bytes 5242880 | tf_op jit(solution)/shard_map/pallas_call | solution.py:349
  17.3 1.3 %collective-permute-start.5 = (f32[2,1,16,128]{3,2,1,0:T(8,128)S(1)}, f32[2,1,16,128]{3,2,1,0:T(8,128)S(1)}, u32[]{:S(2)}, u32[]{:S(2)}) collective-permute-start(f32[2,1,16,128]{3,2,1,0:T(8,128)S(1)} %shard_map.50), channel_id=1, source_target_pairs={{0,5},{1,4},{2,7},{3,6},{4,1},{5,0},{6,3},{7,2},{8,13},{9,12},{10,... | collective-permute-start | bytes 49160 | tf_op jit(solution)/shard_map/ppermute | solution.py:276
  18.7 1.6 %shard_map.49 = f32[2,1,16,128]{3,2,1,0:T(8,128)S(1)} custom-call(bf16[80,128]{1,0:T(8,128)(2,1)S(1)} %constant_dynamic-update-slice_fusion.refs_0_, bf16[64,128]{1,0:T(8,128)(2,1)S(1)} %collective-permute-done.2.refs_1_, f32[16,128]{1,0:T(8,128)S(1)} %shard_map.47.refs_2_, bf16[48,256,128]{2,1,0:T(8,128)(2,1)S(1)} %get-tuple-element.10.refs_3_.refs_2_, ...), custom_call_target="tpu_custom_call" | custom-call | flops 536870912 | bytes 4194304 | tf_op jit(solution)/shard_map/pallas_call | solution.py:357
  20.2 0.3 %collective-permute-done.5 = f32[2,1,16,128]{3,2,1,0:T(8,128)S(1)} collective-permute-done((f32[2,1,16,128]{3,2,1,0:T(8,128)S(1)}, f32[2,1,16,128]{3,2,1,0:T(8,128)S(1)}, u32[]{:S(2)}, u32[]{:S(2)}) %collective-permute-start.5) | collective-permute-done | bytes 16416 | tf_op jit(solution)/shard_map/ppermute | solution.py:276
  20.6 2.4 %collective-permute-start.6 = (f32[1,1,16,128]{3,2,1,0:T(8,128)S(1)}, f32[1,1,16,128]{3,2,1,0:T(8,128)S(1)}, u32[]{:S(2)}, u32[]{:S(2)}) collective-permute-start(f32[1,1,16,128]{3,2,1,0:T(8,128)S(1)} %slice.24), channel_id=1, source_target_pairs={{0,9},{1,8},{2,11},{3,10},{4,13},{5,12},{6,15},{7,14},{8,1},{9,0},... | collective-permute-start | bytes 24584 | tf_op jit(solution)/shard_map/ppermute | solution.py:276
  23.0 1.6 %collective-permute-done.6 = f32[1,1,16,128]{3,2,1,0:T(8,128)S(1)} collective-permute-done((f32[1,1,16,128]{3,2,1,0:T(8,128)S(1)}, f32[1,1,16,128]{3,2,1,0:T(8,128)S(1)}, u32[]{:S(2)}, u32[]{:S(2)}) %collective-permute-start.6) | collective-permute-done | bytes 8224 | tf_op jit(solution)/shard_map/ppermute | solution.py:276
  24.6 1.2 %collective-permute-start.7 = (f32[1,16,128]{2,1,0:T(8,128)S(1)}, f32[1,16,128]{2,1,0:T(8,128)S(1)}, u32[]{:S(2)}, u32[]{:S(2)}) collective-permute-start(f32[1,16,128]{2,1,0:T(8,128)S(1)} %fusion), channel_id=1, source_target_pairs={{0,3},{1,2},{2,1},{3,0},{4,7},{5,6},{6,5},{7,4},{8,11},{9,10},{10,... | collective-permute-start | bytes 24584 | tf_op jit(solution)/shard_map/ppermute | solution.py:276
  25.7 1.9 %collective-permute-done.7 = f32[1,16,128]{2,1,0:T(8,128)S(1)} collective-permute-done((f32[1,16,128]{2,1,0:T(8,128)S(1)}, f32[1,16,128]{2,1,0:T(8,128)S(1)}, u32[]{:S(2)}, u32[]{:S(2)}) %collective-permute-start.7) | collective-permute-done | bytes 8224 | tf_op jit(solution)/shard_map/ppermute | solution.py:276
  27.6 0.2 collective-permute-start.8
  27.8 1.0 %collective-permute-done.8.other_ref = f32[1,16,128]{2,1,0:T(8,128)S(1)} collective-permute-done((f32[1,16,128]{2,1,0:T(8,128)S(1)}, f32[1,16,128]{2,1,0:T(8,128)S(1)}, u32[]{:S(2)}, u32[]{:S(2)}) %collective-permute-start.8) | collective-permute-done | bytes 8224 | tf_op jit(solution)/shard_map/ppermute | solution.py:276
  28.8 0.7 %finish.1 = f32[2,32]{1,0:T(2,128)} custom-call(f32[1,16,128]{2,1,0:T(8,128)S(1)} %max.11.mine_ref, f32[1,16,128]{2,1,0:T(8,128)S(1)} %collective-permute-done.8.other_ref), custom_call_target="tpu_custom_call" | custom-call | tf_op jit(solution)/shard_map/finish/pallas_call | solution.py:375
  (12 shorter events, 0.1 us)
Async XLA Ops:
  0.0 4.4 %collective-permute-start = (bf16[16,128]{1,0:T(8,128)(2,1)}, bf16[16,128]{1,0:T(8,128)(2,1)S(1)}, u32[]{:S(2)}, u32[]{:S(2)}) collective-permute-start(bf16[16,128]{1,0:T(8,128)(2,1)} %bitcast.7), channel_id=1, source_target_pairs={{0,3},{1,2},{2,1},{3,0},{4,7},{5,6},{6,5},{7,4},{8,11},{9,10},{10,... | collective-permute-start | bytes 12296 | tf_op jit(solution)/shard_map/ppermute | solution.py:276
  4.4 4.3 %collective-permute-start.1 = (bf16[40,128]{1,0:T(8,128)(2,1)S(1)}, bf16[40,128]{1,0:T(8,128)(2,1)S(1)}, u32[]{:S(2)}, u32[]{:S(2)}) collective-permute-start(bf16[40,128]{1,0:T(8,128)(2,1)S(1)} %pad_maximum_fusion.1), channel_id=1, source_target_pairs={{0,9},{1,8},{2,11},{3,10},{4,13},{5,12},{6,15},{7,14},{8,1},{9,0},... | collective-permute-start | bytes 30728 | tf_op jit(solution)/shard_map/ppermute | solution.py:276
  8.8 3.3 %collective-permute-start.3 = (bf16[80,128]{1,0:T(8,128)(2,1)S(1)}, bf16[80,128]{1,0:T(8,128)(2,1)S(1)}, u32[]{:S(2)}, u32[]{:S(2)}) collective-permute-start(bf16[80,128]{1,0:T(8,128)(2,1)S(1)} %constant_dynamic-update-slice_fusion.refs_0_), channel_id=1, source_target_pairs={{0,5},{1,4},{2,7},{3,6},{4,1},{5,0},{6,3},{7,2},{8,13},{9,12},{10,... | collective-permute-start | bytes 61448 | tf_op jit(solution)/shard_map/ppermute | solution.py:276
  10.4 4.5 %collective-permute-start.2 = (bf16[64,128]{1,0:T(8,128)(2,1)S(1)}, bf16[64,128]{1,0:T(8,128)(2,1)S(1)}, u32[]{:S(2)}, u32[]{:S(2)}) collective-permute-start(bf16[64,128]{1,0:T(8,128)(2,1)S(1)} %pad_maximum_fusion), channel_id=1, source_target_pairs={{0,1},{1,0},{2,3},{3,2},{4,5},{5,4},{6,7},{7,6},{8,9},{9,8},{10,11... | collective-permute-start | bytes 49160 | tf_op jit(solution)/shard_map/ppermute | solution.py:276
  12.0 3.4 %collective-permute-start.4 = (bf16[64,128]{1,0:T(8,128)(2,1)S(1)}, bf16[64,128]{1,0:T(8,128)(2,1)S(1)}, u32[]{:S(2)}, u32[]{:S(2)}) collective-permute-start(bf16[64,128]{1,0:T(8,128)(2,1)S(1)} %slice.22), channel_id=1, source_target_pairs={{0,1},{1,0},{2,3},{3,2},{4,5},{5,4},{6,7},{7,6},{8,9},{9,8},{10,11... | collective-permute-start | bytes 49160 | tf_op jit(solution)/shard_map/ppermute | solution.py:276
  17.3 3.2 %collective-permute-start.5 = (f32[2,1,16,128]{3,2,1,0:T(8,128)S(1)}, f32[2,1,16,128]{3,2,1,0:T(8,128)S(1)}, u32[]{:S(2)}, u32[]{:S(2)}) collective-permute-start(f32[2,1,16,128]{3,2,1,0:T(8,128)S(1)} %shard_map.50), channel_id=1, source_target_pairs={{0,5},{1,4},{2,7},{3,6},{4,1},{5,0},{6,3},{7,2},{8,13},{9,12},{10,... | collective-permute-start | bytes 49160 | tf_op jit(solution)/shard_map/ppermute | solution.py:276
  20.6 4.0 %collective-permute-start.6 = (f32[1,1,16,128]{3,2,1,0:T(8,128)S(1)}, f32[1,1,16,128]{3,2,1,0:T(8,128)S(1)}, u32[]{:S(2)}, u32[]{:S(2)}) collective-permute-start(f32[1,1,16,128]{3,2,1,0:T(8,128)S(1)} %slice.24), channel_id=1, source_target_pairs={{0,9},{1,8},{2,11},{3,10},{4,13},{5,12},{6,15},{7,14},{8,1},{9,0},... | collective-permute-start | bytes 24584 | tf_op jit(solution)/shard_map/ppermute | solution.py:276
  24.6 3.1 %collective-permute-start.7 = (f32[1,16,128]{2,1,0:T(8,128)S(1)}, f32[1,16,128]{2,1,0:T(8,128)S(1)}, u32[]{:S(2)}, u32[]{:S(2)}) collective-permute-start(f32[1,16,128]{2,1,0:T(8,128)S(1)} %fusion), channel_id=1, source_target_pairs={{0,3},{1,2},{2,1},{3,0},{4,7},{5,6},{6,5},{7,4},{8,11},{9,10},{10,... | collective-permute-start | bytes 24584 | tf_op jit(solution)/shard_map/ppermute | solution.py:276
  27.6 1.2 %collective-permute-start.8 = (f32[1,16,128]{2,1,0:T(8,128)S(1)}, f32[1,16,128]{2,1,0:T(8,128)S(1)}, u32[]{:S(2)}, u32[]{:S(2)}) collective-permute-start(f32[1,16,128]{2,1,0:T(8,128)S(1)} %max.11.mine_ref), channel_id=1, source_target_pairs={{0,1},{1,0},{2,3},{3,2},{4,5},{5,4},{6,7},{7,6},{8,9},{9,8},{10,11... | collective-permute-start | bytes 24584 | tf_op jit(solution)/shard_map/ppermute | solution.py:276
